TPU v7x, 256 devices: a whole 4x4x8 slice. The times are simulated.
256 devices in a mesh: vol: 64 (over z, y, core), dsg: 4 (over x).
Axes of the slice: x: 4, y: 4, z: 8, core: 2. Of those that a mesh axis runs over, the one named last changes fastest.
Arguments:
- fields: float32 [262144, 128], P('vol'), may hold values from -6 to 6
- far_geom: float32 [8, 131072], P(None, ('vol', 'dsg')), may hold values from -6 to 6, as said below
- far_block: int32 [131072, 1], P(('vol', 'dsg')), may hold values from 0 to 63; in each aligned block of 512 rows (0 to 511, 512 to 1023, ...) at most 20 rows name the same one
- far_cell: int32 [131072], P(('vol', 'dsg')), may hold values from 0 to 4095
- far_patch: int32 [131072], P(('vol', 'dsg')), may hold values from 0 to 95, as said below
- near_geom: float32 [8, 524288], P(None, ('vol', 'dsg')), may hold values from -6 to 6, as said below
- near_cell: int32 [524288], P(('vol', 'dsg')), may hold values from 0 to 4095
- near_patch: int32 [524288], P(('vol', 'dsg')), may hold values from 0 to 95, as said below
- adjacency: int32 [96, 4], replicated, may hold values from -1 to 95, as said below
Outputs:
- far_density: float32 [131072], P(('vol', 'dsg'))
- design_grad: float32 [96, 64, 64], P('dsg')
Inputs may be any that keep to these rules, and one draw needn't show every extreme that they name: `far_geom`: rows 0-2 and 6-7 lie in [0, 1). `near_geom`: rows 0-2 and 6-7 lie in [0, 1). `far_block`: the 512 far points of one device name each block at most 20 times. `far_patch`: the far and near points of one device lie on at most 4 design patches, the same set for both. `near_patch`: the far and near points of one device lie on at most 4 design patches, the same set for both. -1 marks a free side; where adjacency[k, s] = m >= 0, adjacency[m, s xor 1] = k.
All inputs are finite; a program needn't handle non-finite values.
Results may differ from a plain program's by a relative error of at most 0.0003.
Values sent between devices are 32-bit elements; how exact they have to be, the bound alone decides.
A program may use at most 128 MiB of HBM per device.

v0:
```python
import jax
import jax.numpy as jnp
import numpy as np
from jax import lax
from jax.sharding import PartitionSpec as P

CTRL = 64
PATCH_GRP = 4
SMOOTH_ITERS = 3
PENALTY = 4.0
SMOOTHING = 16.0
FLIPPED = np.array([1, 0, 3, 2], dtype=np.int32)


def bernstein(position):
    complement = 1.0 - position
    values = jnp.stack(
        [
            complement * complement * complement,
            3.0 * position * complement * complement,
            3.0 * position * position * complement,
            position * position * position,
        ]
    )
    slopes = jnp.stack(
        [
            -3.0 * complement * complement,
            3.0 * complement * complement - 6.0 * position * complement,
            6.0 * position * complement - 3.0 * position * position,
            3.0 * position * position,
        ]
    )
    return (values, slopes)


def tensor_basis(factor_x, factor_y, factor_z):
    product = factor_x[:, None, None, :] * factor_y[None, :, None, :] * factor_z[None, None, :, :]
    return product.reshape(-1, factor_x.shape[-1])


def evaluate(columns, coords):
    value_x, slope_x = bernstein(coords[0])
    value_y, slope_y = bernstein(coords[1])
    value_z, slope_z = bernstein(coords[2])
    basis_set = [
        tensor_basis(value_x, value_y, value_z),
        tensor_basis(slope_x, value_y, value_z),
        tensor_basis(value_x, slope_y, value_z),
        tensor_basis(value_x, value_y, slope_z),
    ]
    half_width = columns.shape[0] // 2
    state_part = columns[:half_width]
    adjoint_part = columns[half_width:]
    results = [jnp.sum(state_part * basis_kind, 0) for basis_kind in basis_set]
    results = results + [jnp.sum(adjoint_part * basis_kind, 0) for basis_kind in basis_set]
    return jnp.stack(results)


def density(values, normals):
    grad_state = values[1:4]
    grad_adjoint = values[5:8]
    normal_sq = jnp.sum(normals * normals, 0)
    inner_sum = jnp.sum(grad_state * grad_adjoint, 0)
    along_state = jnp.sum(grad_state * normals, 0)
    along_adjoint = jnp.sum(grad_adjoint * normals, 0)
    return (
        normal_sq * inner_sum
        - 2.0 * along_state * along_adjoint
        + PENALTY * normal_sq * values[0] * values[4]
    )


def spline_weights(param, span_count):
    scaled = param * span_count
    first_span = jnp.clip(jnp.floor(scaled), 0, span_count - 1)
    offset_in = scaled - first_span
    complement = 1.0 - offset_in
    cubed = offset_in * offset_in * offset_in
    squared = offset_in * offset_in
    weights = jnp.stack(
        [
            complement * complement * complement / 6.0,
            (3.0 * cubed - 6.0 * squared + 4.0) / 6.0,
            (-3.0 * cubed + 3.0 * squared + 3.0 * offset_in + 1.0) / 6.0,
            cubed / 6.0,
        ]
    )
    return (first_span.astype(jnp.int32), weights)


def spline_matrix(param, control):
    start, weights = spline_weights(param, control - 3)
    columns = jnp.arange(control, dtype=jnp.int32)
    matrix = jnp.zeros((param.shape[0], control), jnp.float32)
    for offset in range(4):
        matrix = matrix + jnp.where(
            (start + offset)[:, None] == columns[None, :], weights[offset][:, None], 0.0
        )
    return matrix


def local_grid(strength, spline_params, patch_ids, slot_ids, slot_live, control):
    weights_s = spline_matrix(spline_params[0], control)
    weights_t = spline_matrix(spline_params[1], control)
    selector = ((patch_ids[:, None] == slot_ids[None, :]) & slot_live[None, :]).astype(jnp.float32)
    left = ((selector * strength[:, None])[:, :, None] * weights_s[:, None, :]).reshape(
        strength.shape[0], -1
    )
    result = jnp.einsum(
        "na,nb->ab",
        left,
        weights_t,
        precision=lax.Precision.HIGHEST,
        preferred_element_type=jnp.float32,
    )
    return result.reshape(slot_ids.shape[0], control, control)


def edge_table(iterate):
    return jnp.stack([iterate[:, 0, :], iterate[:, -1, :], iterate[:, :, 0], iterate[:, :, -1]], 1)


def lookup(edge_rows, neighbours):
    total_rows = edge_rows.shape[0] * 4
    wanted = (neighbours * 4 + FLIPPED[None, :]).reshape(-1)
    present = (neighbours >= 0).reshape(-1)
    selector = (
        (wanted[:, None] == jnp.arange(total_rows, dtype=jnp.int32)[None, :]) & present[:, None]
    ).astype(jnp.float32)
    picked = jnp.dot(
        selector,
        edge_rows.reshape(total_rows, -1),
        precision=lax.Precision.HIGHEST,
        preferred_element_type=jnp.float32,
    )
    return picked.reshape(neighbours.shape[0], 4, -1)


def apply_operator(iterate, halo_rows):
    patch_count, edge_size = (iterate.shape[0], iterate.shape[1])
    padded = jnp.zeros((patch_count, edge_size + 2, edge_size + 2), iterate.dtype)
    padded = padded.at[:, 1:-1, 1:-1].set(iterate)
    padded = padded.at[:, 0, 1:-1].set(halo_rows[:, 0])
    padded = padded.at[:, -1, 1:-1].set(halo_rows[:, 1])
    padded = padded.at[:, 1:-1, 0].set(halo_rows[:, 2])
    padded = padded.at[:, 1:-1, -1].set(halo_rows[:, 3])
    beside = padded[:, :-2, 1:-1] + padded[:, 2:, 1:-1] + padded[:, 1:-1, :-2] + padded[:, 1:-1, 2:]
    return iterate + SMOOTHING * (4.0 * iterate - beside)


def precondition(residual):
    patch_count, edge_size = (residual.shape[0], residual.shape[1])
    below_diag = jnp.full((patch_count, edge_size), -SMOOTHING, residual.dtype).at[:, 0].set(0.0)
    main_diag = jnp.full((patch_count, edge_size), 1.0 + 2.0 * SMOOTHING, residual.dtype)
    above_diag = jnp.full((patch_count, edge_size), -SMOOTHING, residual.dtype).at[:, -1].set(0.0)
    along_rows = lax.linalg.tridiagonal_solve(below_diag, main_diag, above_diag, residual)
    along_cols = lax.linalg.tridiagonal_solve(
        below_diag, main_diag, above_diag, jnp.swapaxes(along_rows, 1, 2)
    )
    return jnp.swapaxes(along_cols, 1, 2)


def keep_table(edge_rows):
    return edge_rows


def smooth(summed, neighbours, edges_of):
    iterate = precondition(summed)
    for sweep_index in range(SMOOTH_ITERS):
        halo_rows = lookup(edges_of(edge_table(iterate)), neighbours)
        iterate = iterate + precondition(summed - apply_operator(iterate, halo_rows))
    return iterate


def per_device(
    fields, far_geom, far_block, far_cell, far_patch, near_geom, near_cell, near_patch, adjacency
):
    vol_count = lax.axis_size("vol")
    far_count = far_cell.shape[0]
    capacity = 5 * far_count // (2 * vol_count)
    patches = adjacency.shape[0]
    control = CTRL
    group = PATCH_GRP
    patch_range = jnp.arange(patches, dtype=jnp.int32)
    present = jnp.any(near_patch[:, None] == patch_range[None, :], 0)
    present = present | jnp.any(far_patch[:, None] == patch_range[None, :], 0)
    rank = jnp.cumsum(present.astype(jnp.int32)) - 1
    matches = present[None, :] & (rank[None, :] == jnp.arange(group, dtype=jnp.int32)[:, None])
    slot_ids = jnp.sum(matches.astype(jnp.int32) * patch_range[None, :], 1)
    slot_live = jnp.any(matches, 1)
    near_count = near_cell.shape[0]
    block_len = min(4096, near_count)
    blocks = near_count // block_len

    def near_block(carried, inputs):
        geom_part, cells_part, patch_part = inputs
        rows = jnp.take(fields, cells_part, axis=0).T
        strength = density(evaluate(rows, geom_part[0:3]), geom_part[3:6])
        return (
            carried
            + local_grid(strength, geom_part[6:8], patch_part, slot_ids, slot_live, control),
            None,
        )

    start_grid = jnp.zeros((group, control, control), jnp.float32)
    grid_local, unused = lax.scan(
        near_block,
        start_grid,
        (
            near_geom.reshape(8, blocks, block_len).transpose(1, 0, 2),
            near_cell.reshape(blocks, block_len),
            near_patch.reshape(blocks, block_len),
        ),
    )
    target = far_block[:, 0]
    onehot_dest = (target[:, None] == jnp.arange(vol_count, dtype=jnp.int32)[None, :]).astype(
        jnp.int32
    )
    before = jnp.cumsum(onehot_dest, 0) - onehot_dest
    slot_rank = jnp.sum(before * onehot_dest, 1)
    slot_of = target * capacity + slot_rank
    request = jnp.zeros((1, vol_count * capacity), jnp.int32).at[0, slot_of].set(far_cell)
    request = request.reshape(1, vol_count, capacity)
    incoming = lax.all_to_all(request, "vol", split_axis=1, concat_axis=1, tiled=True)
    picked = jnp.take(fields, incoming.reshape(-1), axis=0).T
    picked = picked.reshape(fields.shape[1], incoming.shape[1], incoming.shape[2])
    replies = lax.all_to_all(picked, "vol", split_axis=1, concat_axis=1, tiled=True)
    placed = jnp.zeros((3, vol_count * capacity), jnp.float32).at[:, slot_of].set(far_geom[0:3])
    slot_values = evaluate(replies.reshape(replies.shape[0], -1), placed)
    far_values = jnp.take(slot_values, slot_of, axis=1)
    far_strength = density(far_values, far_geom[3:6])
    grid_local = grid_local + local_grid(
        far_strength, far_geom[6:8], far_patch, slot_ids, slot_live, control
    )
    placing = ((patch_range[:, None] == slot_ids[None, :]) & slot_live[None, :]).astype(jnp.float32)
    owner_count = lax.axis_size("dsg")
    per_owner = patches // owner_count
    owner_index = lax.axis_index("dsg")
    grid_whole = jnp.dot(
        placing,
        grid_local.reshape(group, -1),
        precision=lax.Precision.HIGHEST,
        preferred_element_type=jnp.float32,
    )
    summed = lax.psum(grid_whole, ("vol", "dsg")).reshape(patches, control, control)
    design = smooth(summed, adjacency, keep_table)
    design = lax.dynamic_slice_in_dim(design, owner_index * per_owner, per_owner, 0)
    return (far_strength, design)


def solution(mesh):
    return jax.shard_map(
        per_device,
        mesh=mesh,
        in_specs=(
            P("vol", None),
            P(None, ("vol", "dsg")),
            P(("vol", "dsg"), None),
            P(("vol", "dsg")),
            P(("vol", "dsg")),
            P(None, ("vol", "dsg")),
            P(("vol", "dsg")),
            P(("vol", "dsg")),
            P(),
        ),
        out_specs=(P(("vol", "dsg")), P("dsg", None, None)),
        check_vma=False,
    )
```

profile of v0, /device:TPU:2, one launch (start us, length us, event | category | flops | bytes accessed | tf_op | source)
XLA Modules:
  0.0 598.5 jit_solution(6945396377052510805)
XLA Ops:
  14.9 12.1 %all-to-all-start = ((s32[1,64,20]{2,0,1:T(1,128)}), s32[1,64,20]{2,0,1:T(1,128)S(1)}, u32[]{:S(2)}, u32[]{:S(2)}) async-start(s32[1,64,20]{2,0,1:T(1,128)} %bitcast.5), calls=%async_computation | async-start | bytes 65536 | tf_op jit(solution)/shard_map/all_to_all | solution.py:224
  68.9 4.6 mul.70848
  73.6 3.5 copy.7280
  77.1 4.4 mul.70860
  81.5 3.6 copy.7281
  85.1 4.4 mul.70872
  89.6 3.6 copy.7282
  93.1 3.8 mul.70882
  96.9 3.5 copy.7283
  100.7 7.6 %gather_fusion.2 = f32[2048,128]{1,0:T(8,128)} fusion(f32[4096,128]{1,0:T(8,128)S(1)} %copy-done, s32[2048]{0:T(1024)S(1)} %get-tuple-element.1882), kind=kCustom, calls=%fused_computation.2 | custom fusion | bytes 2105344 | tf_op jit(solution)/shard_map/while/body/eval_jaxpr/jit(_take)/gather | solution.py:197
  108.4 3.1 gather_fusion
  115.1 10.4 %all-to-all-start.1 = ((f32[128,64,20]{0,2,1:T(8,128)}), f32[128,64,20]{0,2,1:T(8,128)S(1)}, u32[]{:S(2)}, u32[]{:S(2)}) async-start(f32[128,64,20]{0,2,1:T(8,128)} %reshape.315135), calls=%async_computation.1 | async-start | bytes 1572864 | tf_op jit(solution)/shard_map/all_to_all | solution.py:227
  130.8 18.1 %all-to-all-done.1 = f32[128,64,20]{0,2,1:T(8,128)S(1)} async-done(((f32[128,64,20]{0,2,1:T(8,128)}), f32[128,64,20]{0,2,1:T(8,128)S(1)}, u32[]{:S(2)}, u32[]{:S(2)}) %all-to-all-start.1) | async-done | bytes 655392 | tf_op jit(solution)/shard_map/all_to_all | solution.py:227
  148.8 3.8 multiply_reduce_fusion.8
  163.0 257.5 %all-reduce.6.cloned.1.call-done = f32[96,64,64]{0,2,1:T(8,128)} async-done(((f32[96,64,64]{0,2,1:T(8,128)}), f32[96,64,64]{0,2,1:T(8,128)}) %all-reduce.6.cloned.1.call-update) | async-done | bytes 1572880 | tf_op jit(solution)/shard_map/psum | solution.py:245
  437.5 4.8 multiply_subtract_fusion.370
  442.4 9.9 %concatenate.199 = f32[63,96,64]{1,0,2:T(8,128)S(1)} concatenate(f32[1,96,64]{1,0,2:T(1,128)} %get-tuple-element.1225, f32[1,96,64]{1,0,2:T(1,128)} %get-tuple-element.1226, f32[1,96,64]{1,0,2:T(1,128)} %get-tuple-element.1227, f32[1,96,64]{1,0,2:T(1,128)} %get-tuple-element.1228, f32[1,96,64]{1,0,2:T(1,128)} %get-tuple-element.1229, f32[1,96,64]{1,0,2:T(1,128)} %get-tuple-element.1230, ...), dimensions={0} | concatenate | bytes 3096576 | tf_op jit(solution)/shard_map/vmap()/concatenate | solution.py:156
  463.7 3.3 fusion.11
  515.1 4.7 multiply_subtract_fusion.124
  519.8 15.6 %concatenate.207 = f32[63,96,64]{1,0,2:T(8,128)} concatenate(f32[1,96,64]{1,0,2:T(1,128)S(1)} %get-tuple-element.820, f32[1,96,64]{1,0,2:T(1,128)S(1)} %get-tuple-element.821, f32[1,96,64]{1,0,2:T(1,128)S(1)} %get-tuple-element.822, f32[1,96,64]{1,0,2:T(1,128)} %get-tuple-element.823, f32[1,96,64]{1,0,2:T(1,128)} %get-tuple-element.824, f32[1,96,64]{1,0,2:T(1,128)} %get-tuple-element.825, ...), dimensions={0} | concatenate | bytes 3096576 | tf_op jit(solution)/shard_map/vmap()/concatenate | solution.py:156
  552.6 4.3 multiply_subtract_fusion.62
  569.4 4.9 multiply_subtract_fusion
  574.4 9.8 %concatenate.211 = f32[63,96,64]{1,0,2:T(8,128)S(1)} concatenate(f32[1,96,64]{1,0,2:T(1,128)S(1)} %get-tuple-element.656, f32[1,96,64]{1,0,2:T(1,128)S(1)} %get-tuple-element.657, f32[1,96,64]{1,0,2:T(1,128)S(1)} %get-tuple-element.658, f32[1,96,64]{1,0,2:T(1,128)} %get-tuple-element.659, f32[1,96,64]{1,0,2:T(1,128)} %get-tuple-element.660, f32[1,96,64]{1,0,2:T(1,128)} %get-tuple-element.661, ...), dimensions={0} | concatenate | bytes 3096576 | tf_op jit(solution)/shard_map/vmap()/concatenate | solution.py:156
  588.2 3.2 copy.8826
  (902 shorter events, 173.5 us)
Async XLA Ops:
  7.2 93.6 %copy-start = (f32[4096,128]{1,0:T(8,128)S(1)}, f32[4096,128]{1,0:T(8,128)}, u32[]{:S(2)}) copy-start(f32[4096,128]{1,0:T(8,128)} %param.58) | copy-start | bytes 6291460
  11.5 30.1 %copy-start.118 = (s32[512,1]{0,1:T(1,128)}, s32[512,1]{0,1:T(1,128)S(1)}, u32[]{:S(2)}) copy-start(s32[512,1]{0,1:T(1,128)S(1)} %get-tuple-element.1367) | copy-start | bytes 6148
  14.9 85.7 %all-to-all-start = ((s32[1,64,20]{2,0,1:T(1,128)}), s32[1,64,20]{2,0,1:T(1,128)S(1)}, u32[]{:S(2)}, u32[]{:S(2)}) async-start(s32[1,64,20]{2,0,1:T(1,128)} %bitcast.5), calls=%async_computation | async-start | bytes 65536 | tf_op jit(solution)/shard_map/all_to_all | solution.py:224
  48.9 4.5 copy-start.119
  93.1 7.3 %copy-start.102 = (f32[3,512]{1,0:T(4,128)S(1)}, f32[3,512]{1,0:T(4,128)}, u32[]{:S(2)}) copy-start(f32[3,512]{1,0:T(4,128)} %get-tuple-element.1815) | copy-start | bytes 18436
  112.9 13.2 %copy-start.109 = (pred[2048]{0:T(1024)(128)(4,1)S(1)}, pred[2048]{0:T(1024)(128)(4,1)}, u32[]{:S(2)}) copy-start(pred[2048]{0:T(1024)(128)(4,1)} %compare_and_fusion) | copy-start | bytes 6148
  115.1 12.6 %copy-start.8 = (f32[64,2048]{0,1:T(8,128)S(1)}, f32[64,2048]{0,1:T(8,128)}, u32[]{:S(2)}) copy-start(f32[64,2048]{0,1:T(8,128)} %copy.7291) | copy-start | bytes 1572868
  115.1 33.7 %all-to-all-start.1 = ((f32[128,64,20]{0,2,1:T(8,128)}), f32[128,64,20]{0,2,1:T(8,128)S(1)}, u32[]{:S(2)}, u32[]{:S(2)}) async-start(f32[128,64,20]{0,2,1:T(8,128)} %reshape.315135), calls=%async_computation.1 | async-start | bytes 1572864 | tf_op jit(solution)/shard_map/all_to_all | solution.py:227
  125.6 294.9 %all-reduce.6.cloned.1.call-start = ((), (), s32[]{:S(2)}) async-start(), calls=%async_computation.2 | async-start | bytes 4194304 | tf_op jit(solution)/shard_map/psum | solution.py:245
  130.8 24.3 %copy-start.133 = (pred[512]{0:T(512)(128)(4,1)S(1)}, pred[512]{0:T(512)(128)(4,1)}, u32[]{:S(2)}) copy-start(pred[512]{0:T(512)(128)(4,1)} %get-tuple-element.1366) | copy-start | bytes 1540
  156.1 6.2 %copy-start.122 = (f32[512]{0:T(512)}, f32[512]{0:T(512)S(1)}, u32[]{:S(2)}) copy-start(f32[512]{0:T(512)S(1)} %multiply_add_fusion.2) | copy-start | bytes 6148
  431.2 11.1 %copy-start.80 = (f32[96,64]{0,1:T(8,128)}, f32[96,64]{0,1:T(8,128)S(1)}, u32[]{:S(2)}) copy-start(f32[96,64]{0,1:T(8,128)S(1)} %get-tuple-element.1210) | copy-start | bytes 73732
  431.2 11.1 %copy-start.83 = (f32[96,64]{0,1:T(8,128)}, f32[96,64]{0,1:T(8,128)S(1)}, u32[]{:S(2)}) copy-start(f32[96,64]{0,1:T(8,128)S(1)} %get-tuple-element.1211) | copy-start | bytes 73732
  431.2 21.0 %copy-start.75 = (f32[96,64]{0,1:T(8,128)}, f32[96,64]{0,1:T(8,128)S(1)}, u32[]{:S(2)}) copy-start(f32[96,64]{0,1:T(8,128)S(1)} %get-tuple-element.1202) | copy-start | bytes 73732
  437.3 5.0 copy-start.11
  437.4 4.9 copy-start.15
  437.4 4.9 copy-start.19
  437.4 4.9 copy-start.23
  437.4 4.9 copy-start.27
  437.5 4.9 copy-start.31
  519.8 15.6 %copy-start.5 = (f32[96,64,64]{0,2,1:T(8,128)S(1)}, f32[96,64,64]{0,2,1:T(8,128)}, u32[]{:S(2)}) copy-start(f32[96,64,64]{0,2,1:T(8,128)} %copy-done.4) | copy-start | bytes 4718596
  519.8 15.6 %copy-start.86 = (f32[96,64]{0,1:T(8,128)S(1)}, f32[96,64]{0,1:T(8,128)}, u32[]{:S(2)}) copy-start(f32[96,64]{0,1:T(8,128)} %get-tuple-element.800) | copy-start | bytes 73732
  574.4 9.8 %copy-start.85 = (f32[96,64]{0,1:T(8,128)S(1)}, f32[96,64]{0,1:T(8,128)}, u32[]{:S(2)}) copy-start(f32[96,64]{0,1:T(8,128)} %get-tuple-element.636) | copy-start | bytes 73732
  585.8 5.6 copy-start.1
  (122 other events, 268.0 us)
Sparse Core Ops, SparseCore 0:
  162.4 258.0 all-reduce.5
where the time goes:
time: 609 us; the launch traced here: 599 us
  waiting for transfers between devices  276 us (45%)
  local copies, waits for them, and re-layouts  155 us (25%)
  other arithmetic  114 us (19%)
  starting transfers between devices  23 us (4%)
  between operations  20.4 us (3%)
  matrix products  10.6 us (2%)
    psum x1, waiting for transfers between devices, per_device(): lax.psum(grid_whole, ('vol', 'dsg')).reshape(patches, control, control)  258 us
    mul x16, local copies, waits for them, and re-layouts, tensor_basis(): factor_x[:, None, None, :] * factor_y[None, :, None, :]  47 us
    sub x37, other arithmetic, precondition(): lax.linalg.tridiagonal_solve(below_diag, main_diag, above_diag, residual)  42 us
    concatenate x3, local copies, waits for them, and re-layouts, precondition(): lax.linalg.tridiagonal_solve(below_diag, main_diag, above_diag, residual)  35.3 us
    all_to_all x1, waiting for transfers between devices, per_device(): lax.all_to_all(picked, 'vol', split_axis=1, concat_axis=1, tiled=True)  18.1 us
    unnamed x515, local copies, waits for them, and re-layouts  16 us
  transfers between devices with their start and end apart: 3, of which 2 were waited for; matrix products, arithmetic and copies ran while one was open for 13% of the time, Pallas kernels for 0%

commit v1 on v0

--- a/solution.py
+++ b/solution.py
@@ -10,6 +10,12 @@
 PENALTY = 4.0
 SMOOTHING = 16.0
 FLIPPED = np.array([1, 0, 3, 2], dtype=np.int32)
+store_cycles = lambda message, comm_axis: jnp.concatenate(
+    lax.all_to_all(
+        jnp.stack(jnp.split(message, lax.psum(1, comm_axis), axis=1), axis=0), comm_axis, 0, 0
+    ),
+    axis=1,
+)
 
 
 def bernstein(position):
@@ -221,7 +227,7 @@
     slot_of = target * capacity + slot_rank
     request = jnp.zeros((1, vol_count * capacity), jnp.int32).at[0, slot_of].set(far_cell)
     request = request.reshape(1, vol_count, capacity)
-    incoming = lax.all_to_all(request, "vol", split_axis=1, concat_axis=1, tiled=True)
+    incoming = store_cycles(request, "vol")
     picked = jnp.take(fields, incoming.reshape(-1), axis=0).T
     picked = picked.reshape(fields.shape[1], incoming.shape[1], incoming.shape[2])
     replies = lax.all_to_all(picked, "vol", split_axis=1, concat_axis=1, tiled=True)

time: 609 us -> 644 us (1.057)
  local copies, waits for them, and re-layouts: 155 us -> 189 us
    unnamed x515 -> x578, local copies, waits for them, and re-layouts: 16 us -> 50.3 us
  transfers between devices with their start and end apart: 3 -> 3, of which waited for: 2 -> 2; matrix products, arithmetic and copies ran while one was open for 13% -> 12% of each run, Pallas kernels for 0% -> 0%
where the time goes in v1:
time: 644 us; the launch traced here: 633 us
  waiting for transfers between devices  275 us (43%)
  local copies, waits for them, and re-layouts  189 us (29%)
  other arithmetic  114 us (18%)
  starting transfers between devices  23 us (4%)
  between operations  20.4 us (3%)
  matrix products  10.6 us (2%)
    psum x1, waiting for transfers between devices, per_device(): lax.psum(grid_whole, ('vol', 'dsg')).reshape(patches, control, control)  257 us
    unnamed x578, local copies, waits for them, and re-layouts  50.3 us
    mul x16, local copies, waits for them, and re-layouts, tensor_basis(): factor_x[:, None, None, :] * factor_y[None, :, None, :]  47 us
    sub x37, other arithmetic, precondition(): lax.linalg.tridiagonal_solve(below_diag, main_diag, above_diag, residual)  42 us
    concatenate x3, local copies, waits for them, and re-layouts, precondition(): lax.linalg.tridiagonal_solve(below_diag, main_diag, above_diag, residual)  35.3 us
    all_to_all x1, waiting for transfers between devices, per_device(): lax.all_to_all(picked, 'vol', split_axis=1, concat_axis=1, tiled=True)  18.1 us
  transfers between devices with their start and end apart: 3, of which 2 were waited for; matrix products, arithmetic and copies ran while one was open for 12% of the time, Pallas kernels for 0%

profile of v1, /device:TPU:2, one launch (start us, length us, event | category | flops | bytes accessed | tf_op | source)
XLA Modules:
  0.0 632.6 jit_solution(12258100428108970044)
XLA Ops:
  49.1 12.1 %all-to-all-start = ((s32[64,1,1,20]{3,2,1,0:T(1,128)}), s32[64,1,1,20]{3,2,1,0:T(1,128)S(1)}, u32[]{:S(2)}, u32[]{:S(2)}) async-start(s32[64,1,1,20]{3,2,1,0:T(1,128)} %constant_dynamic-update-slice_fusion), calls=%async_computation | async-start | bytes 65536 | tf_op jit(solution)/shard_map/all_to_all | solution.py:14
  103.2 4.6 mul.70848
  107.8 3.5 copy.10669
  111.3 4.4 mul.70860
  115.7 3.6 copy.10670
  119.3 4.4 mul.70872
  123.8 3.6 copy.10671
  127.3 3.8 mul.70882
  131.1 3.5 copy.10672
  135.0 7.6 %gather_fusion.2 = f32[2048,128]{1,0:T(8,128)} fusion(f32[4096,128]{1,0:T(8,128)S(1)} %copy-done, s32[2048]{0:T(1024)S(1)} %get-tuple-element.1886), kind=kCustom, calls=%fused_computation.2 | custom fusion | bytes 2105344 | tf_op jit(solution)/shard_map/while/body/eval_jaxpr/jit(_take)/gather | solution.py:203
  142.6 3.1 gather_fusion
  149.3 10.4 %all-to-all-start.1 = ((f32[128,64,20]{0,2,1:T(8,128)}), f32[128,64,20]{0,2,1:T(8,128)S(1)}, u32[]{:S(2)}, u32[]{:S(2)}) async-start(f32[128,64,20]{0,2,1:T(8,128)} %reshape.315128), calls=%async_computation.1 | async-start | bytes 1572864 | tf_op jit(solution)/shard_map/all_to_all | solution.py:233
  165.0 18.1 %all-to-all-done.1 = f32[128,64,20]{0,2,1:T(8,128)S(1)} async-done(((f32[128,64,20]{0,2,1:T(8,128)}), f32[128,64,20]{0,2,1:T(8,128)S(1)}, u32[]{:S(2)}, u32[]{:S(2)}) %all-to-all-start.1) | async-done | bytes 655392 | tf_op jit(solution)/shard_map/all_to_all | solution.py:233
  183.0 3.8 multiply_reduce_fusion.8
  197.2 257.4 %all-reduce.6.cloned.1.call-done = f32[96,64,64]{0,2,1:T(8,128)} async-done(((f32[96,64,64]{0,2,1:T(8,128)}), f32[96,64,64]{0,2,1:T(8,128)}) %all-reduce.6.cloned.1.call-update) | async-done | bytes 1572880 | tf_op jit(solution)/shard_map/psum | solution.py:251
  471.5 4.8 multiply_subtract_fusion.370
  476.4 9.9 %concatenate.199 = f32[63,96,64]{1,0,2:T(8,128)S(1)} concatenate(f32[1,96,64]{1,0,2:T(1,128)} %get-tuple-element.1229, f32[1,96,64]{1,0,2:T(1,128)} %get-tuple-element.1230, f32[1,96,64]{1,0,2:T(1,128)} %get-tuple-element.1231, f32[1,96,64]{1,0,2:T(1,128)} %get-tuple-element.1232, f32[1,96,64]{1,0,2:T(1,128)} %get-tuple-element.1233, f32[1,96,64]{1,0,2:T(1,128)} %get-tuple-element.1234, ...), dimensions={0} | concatenate | bytes 3096576 | tf_op jit(solution)/shard_map/vmap()/concatenate | solution.py:162
  497.8 3.3 fusion.11
  549.2 4.7 multiply_subtract_fusion.124
  553.9 15.6 %concatenate.207 = f32[63,96,64]{1,0,2:T(8,128)} concatenate(f32[1,96,64]{1,0,2:T(1,128)S(1)} %get-tuple-element.824, f32[1,96,64]{1,0,2:T(1,128)S(1)} %get-tuple-element.825, f32[1,96,64]{1,0,2:T(1,128)S(1)} %get-tuple-element.826, f32[1,96,64]{1,0,2:T(1,128)} %get-tuple-element.827, f32[1,96,64]{1,0,2:T(1,128)} %get-tuple-element.828, f32[1,96,64]{1,0,2:T(1,128)} %get-tuple-element.829, ...), dimensions={0} | concatenate | bytes 3096576 | tf_op jit(solution)/shard_map/vmap()/concatenate | solution.py:162
  586.6 4.3 multiply_subtract_fusion.62
  603.5 4.9 multiply_subtract_fusion
  608.4 9.8 %concatenate.211 = f32[63,96,64]{1,0,2:T(8,128)S(1)} concatenate(f32[1,96,64]{1,0,2:T(1,128)S(1)} %get-tuple-element.660, f32[1,96,64]{1,0,2:T(1,128)S(1)} %get-tuple-element.661, f32[1,96,64]{1,0,2:T(1,128)S(1)} %get-tuple-element.662, f32[1,96,64]{1,0,2:T(1,128)} %get-tuple-element.663, f32[1,96,64]{1,0,2:T(1,128)} %get-tuple-element.664, f32[1,96,64]{1,0,2:T(1,128)} %get-tuple-element.665, ...), dimensions={0} | concatenate | bytes 3096576 | tf_op jit(solution)/shard_map/vmap()/concatenate | solution.py:162
  622.3 3.2 copy.12215
  (966 shorter events, 207.7 us)
Async XLA Ops:
  7.2 127.8 %copy-start = (f32[4096,128]{1,0:T(8,128)S(1)}, f32[4096,128]{1,0:T(8,128)}, u32[]{:S(2)}) copy-start(f32[4096,128]{1,0:T(8,128)} %param.58) | copy-start | bytes 6291460
  11.5 64.3 %copy-start.118 = (s32[512,1]{0,1:T(1,128)}, s32[512,1]{0,1:T(1,128)S(1)}, u32[]{:S(2)}) copy-start(s32[512,1]{0,1:T(1,128)S(1)} %get-tuple-element.1371) | copy-start | bytes 6148
  49.1 85.7 %all-to-all-start = ((s32[64,1,1,20]{3,2,1,0:T(1,128)}), s32[64,1,1,20]{3,2,1,0:T(1,128)S(1)}, u32[]{:S(2)}, u32[]{:S(2)}) async-start(s32[64,1,1,20]{3,2,1,0:T(1,128)} %constant_dynamic-update-slice_fusion), calls=%async_computation | async-start | bytes 65536 | tf_op jit(solution)/shard_map/all_to_all | solution.py:14
  83.1 4.5 copy-start.119
  127.3 7.3 %copy-start.102 = (f32[3,512]{1,0:T(4,128)S(1)}, f32[3,512]{1,0:T(4,128)}, u32[]{:S(2)}) copy-start(f32[3,512]{1,0:T(4,128)} %get-tuple-element.1819) | copy-start | bytes 18436
  147.1 13.2 %copy-start.109 = (pred[2048]{0:T(1024)(128)(4,1)S(1)}, pred[2048]{0:T(1024)(128)(4,1)}, u32[]{:S(2)}) copy-start(pred[2048]{0:T(1024)(128)(4,1)} %compare_and_fusion) | copy-start | bytes 6148
  149.3 12.6 %copy-start.8 = (f32[64,2048]{0,1:T(8,128)S(1)}, f32[64,2048]{0,1:T(8,128)}, u32[]{:S(2)}) copy-start(f32[64,2048]{0,1:T(8,128)} %copy.10680) | copy-start | bytes 1572868
  149.3 33.7 %all-to-all-start.1 = ((f32[128,64,20]{0,2,1:T(8,128)}), f32[128,64,20]{0,2,1:T(8,128)S(1)}, u32[]{:S(2)}, u32[]{:S(2)}) async-start(f32[128,64,20]{0,2,1:T(8,128)} %reshape.315128), calls=%async_computation.1 | async-start | bytes 1572864 | tf_op jit(solution)/shard_map/all_to_all | solution.py:233
  159.8 294.8 %all-reduce.6.cloned.1.call-start = ((), (), s32[]{:S(2)}) async-start(), calls=%async_computation.2 | async-start | bytes 4194304 | tf_op jit(solution)/shard_map/psum | solution.py:251
  165.0 24.3 %copy-start.133 = (pred[512]{0:T(512)(128)(4,1)S(1)}, pred[512]{0:T(512)(128)(4,1)}, u32[]{:S(2)}) copy-start(pred[512]{0:T(512)(128)(4,1)} %get-tuple-element.1370) | copy-start | bytes 1540
  190.3 6.2 copy-start.122
  465.3 11.1 %copy-start.80 = (f32[96,64]{0,1:T(8,128)}, f32[96,64]{0,1:T(8,128)S(1)}, u32[]{:S(2)}) copy-start(f32[96,64]{0,1:T(8,128)S(1)} %get-tuple-element.1214) | copy-start | bytes 73732
  465.3 11.1 %copy-start.83 = (f32[96,64]{0,1:T(8,128)}, f32[96,64]{0,1:T(8,128)S(1)}, u32[]{:S(2)}) copy-start(f32[96,64]{0,1:T(8,128)S(1)} %get-tuple-element.1215) | copy-start | bytes 73732
  465.3 21.0 %copy-start.75 = (f32[96,64]{0,1:T(8,128)}, f32[96,64]{0,1:T(8,128)S(1)}, u32[]{:S(2)}) copy-start(f32[96,64]{0,1:T(8,128)S(1)} %get-tuple-element.1206) | copy-start | bytes 73732
  471.4 5.0 copy-start.11
  471.4 4.9 copy-start.15
  471.4 4.9 copy-start.19
  471.5 4.9 copy-start.23
  471.5 4.9 copy-start.27
  471.5 4.9 copy-start.31
  553.8 15.6 %copy-start.5 = (f32[96,64,64]{0,2,1:T(8,128)S(1)}, f32[96,64,64]{0,2,1:T(8,128)}, u32[]{:S(2)}) copy-start(f32[96,64,64]{0,2,1:T(8,128)} %copy-done.4) | copy-start | bytes 4718596
  553.8 15.6 %copy-start.86 = (f32[96,64]{0,1:T(8,128)S(1)}, f32[96,64]{0,1:T(8,128)}, u32[]{:S(2)}) copy-start(f32[96,64]{0,1:T(8,128)} %get-tuple-element.804) | copy-start | bytes 73732
  608.4 9.8 %copy-start.85 = (f32[96,64]{0,1:T(8,128)S(1)}, f32[96,64]{0,1:T(8,128)}, u32[]{:S(2)}) copy-start(f32[96,64]{0,1:T(8,128)} %get-tuple-element.640) | copy-start | bytes 73732
  619.9 5.6 copy-start.1
  (122 other events, 268.0 us)
Sparse Core Ops, SparseCore 0:
  196.6 257.9 all-reduce.5
